TPU v7x, 32 devices: a whole 2x2x4 slice. The times are simulated.
32 devices in a mesh: ctx: 8 (over z, x), head: 4 (over y, core).
Axes of the slice: x: 2, y: 2, z: 4, core: 2. Of those that a mesh axis runs over, the one named last changes fastest.
Arguments:
- queries: bfloat16 [4096, 4096], P('ctx', 'head'), may hold values from -5 to 5
- keys: bfloat16 [4096, 512], P('ctx', 'head'), may hold values from -5 to 5
- values: bfloat16 [4096, 512], P('ctx', 'head'), may hold values from -8 to 8
- feature_map: bfloat16 [4, 128, 16], P('head'), may hold values from -0.5 to 0.5
- out_proj: bfloat16 [4096, 8192], P('ctx', 'head'), may hold values from -0.09375 to 0.09375
- teacher: bfloat16 [4096, 8192], P('ctx', 'head'), may hold values from -16 to 16
Outputs:
- student_out: bfloat16 [4096, 8192], P('ctx', 'head')
- loss: float32 [], replicated
- feature_grad: float32 [4, 128, 16], P('head')
All inputs are finite; a program needn't handle non-finite values.
Results may differ from a plain program's by a relative error of at most 0.006.
Values may be sent and summed in bfloat16 or wider, within the bound.
A program may use at most 128 MiB of HBM per device.

v0:
```python
import math
import jax
import jax.numpy as jnp
from jax import lax
from jax.sharding import PartitionSpec as P

D = 8192
HEAD_DIM = 128
GROUP = 8
WIN = 64
exact_mode = lax.Precision.HIGHEST


def shifted(block, axis, distance):
    devices = range(lax.axis_size(axis))
    route = [(i - distance, i) for i in devices if i - distance in devices]
    return lax.ppermute(block, axis, route)


def taylor_square(features):
    feature_count = features.shape[-1]
    outer = features[..., :, None] * features[..., None, :]
    return outer.reshape(features.shape[:-1] + (feature_count * feature_count,))


def square_grad(grad_square, features):
    feature_count = features.shape[-1]
    matrix = grad_square.reshape(features.shape + (feature_count,))
    return jnp.einsum("...fh,...h->...f", matrix, features, precision=exact_mode) + jnp.einsum(
        "...hf,...h->...f", matrix, features, precision=exact_mode
    )


def masked_total(select, member):
    shaped = select.reshape((select.shape[0],) + (1,) * (member.ndim - 1))
    return jnp.sum(jnp.where(shaped, member, jnp.zeros_like(member)), axis=0)


def window_tiles(extended, tok_rows):
    tile_count = tok_rows // WIN
    first = extended[:tok_rows].reshape((tile_count, WIN) + extended.shape[1:])
    second = extended[WIN:].reshape((tile_count, WIN) + extended.shape[1:])
    return jnp.concatenate([first, second], 1)


def local(queries, keys, values, feature_map, out_proj, teacher):
    tok_rows = queries.shape[0]
    kv_groups = keys.shape[1] // HEAD_DIM
    ctx_count = lax.axis_size("ctx")
    ctx_index = lax.axis_index("ctx")
    query_heads = queries.reshape(tok_rows, kv_groups, GROUP, HEAD_DIM)
    key_heads = keys.reshape(tok_rows, kv_groups, HEAD_DIM)
    value_float = values.reshape(tok_rows, kv_groups, HEAD_DIM).astype(jnp.float32)
    query_features = jnp.einsum(
        "tgqe,gef->tgqf", query_heads, feature_map, preferred_element_type=jnp.float32
    )
    key_features = jnp.einsum(
        "tge,gef->tgf", key_heads, feature_map, preferred_element_type=jnp.float32
    )
    rim_rows = shifted(jnp.stack([keys[tok_rows - WIN :], values[tok_rows - WIN :]]), "ctx", 1)
    keys_ext = jnp.concatenate([rim_rows[0], keys], 0).reshape(tok_rows + WIN, kv_groups, HEAD_DIM)
    values_ext = jnp.concatenate([rim_rows[1], values], 0).reshape(
        tok_rows + WIN, kv_groups, HEAD_DIM
    )
    tile_count = tok_rows // WIN
    key_tiles = window_tiles(keys_ext, tok_rows)
    value_tiles = window_tiles(values_ext, tok_rows)
    query_tiles = query_heads.reshape(tile_count, WIN, kv_groups, GROUP, HEAD_DIM)
    scores = jnp.einsum(
        "ntgqe,nsge->ngqts", query_tiles, key_tiles, preferred_element_type=jnp.float32
    ) / math.sqrt(HEAD_DIM)
    tile_pos = lax.broadcasted_iota(jnp.int32, (tile_count, WIN, 2 * WIN), 0)
    query_pos = lax.broadcasted_iota(jnp.int32, (tile_count, WIN, 2 * WIN), 1)
    key_pos = lax.broadcasted_iota(jnp.int32, (tile_count, WIN, 2 * WIN), 2)
    distance = query_pos + WIN - key_pos
    allowed = (
        (distance >= 0)
        & (distance < WIN)
        & (ctx_index * tok_rows + tile_pos * WIN + key_pos - WIN >= 0)
    )
    allowed = allowed[:, None, None]
    scores = jnp.where(allowed, scores, -jnp.inf)
    row_max = jnp.max(scores, axis=-1, keepdims=True)
    weights = jnp.where(allowed, jnp.exp(scores - row_max), 0.0)
    attn_weights = (weights / jnp.sum(weights, axis=-1, keepdims=True)).astype(jnp.bfloat16)
    window_out = jnp.einsum(
        "ngqts,nsge->ntgqe", attn_weights, value_tiles, preferred_element_type=jnp.float32
    ).reshape(tok_rows, kv_groups, GROUP, HEAD_DIM)
    causal = lax.broadcasted_iota(jnp.int32, (tok_rows, tok_rows), 0) >= lax.broadcasted_iota(
        jnp.int32, (tok_rows, tok_rows), 1
    )
    qk_inner = (
        jnp.einsum("tgqf,sgf->gqts", query_features, key_features, precision=exact_mode) / 4.0
    )
    kernel = jnp.where(causal, 1.0 + qk_inner + 0.5 * qk_inner * qk_inner, 0.0)
    numerator = jnp.einsum("gqts,sge->tgqe", kernel, value_float, precision=exact_mode)
    denominator = jnp.transpose(jnp.sum(kernel, axis=-1), (2, 0, 1))
    key_square = taylor_square(key_features)
    own_square_v = jnp.einsum("sgk,sge->gke", key_square, value_float, precision=exact_mode)
    own_linear_v = jnp.einsum("sgf,sge->gfe", key_features, value_float, precision=exact_mode)
    own_values = jnp.sum(value_float, axis=0)
    own_square_k = jnp.sum(key_square, axis=0)
    own_linear_k = jnp.sum(key_features, axis=0)
    own_count = jnp.full((kv_groups,), float(tok_rows), jnp.float32)
    gathered = (
        lax.all_gather(own_square_v[None], "ctx", axis=0, tiled=True),
        lax.all_gather(own_linear_v[None], "ctx", axis=0, tiled=True),
        lax.all_gather(own_values[None], "ctx", axis=0, tiled=True),
        lax.all_gather(own_square_k[None], "ctx", axis=0, tiled=True),
        lax.all_gather(own_linear_k[None], "ctx", axis=0, tiled=True),
        lax.all_gather(own_count[None], "ctx", axis=0, tiled=True),
    )
    lower_select = jnp.arange(ctx_count) < ctx_index
    earlier = tuple((masked_total(lower_select, member) for member in gathered))
    past_square_v, past_linear_v, past_values, past_square_k, past_linear_k, past_count = earlier
    query_square = taylor_square(query_features)
    numerator = (
        numerator
        + jnp.einsum("tgqk,gke->tgqe", query_square, past_square_v, precision=exact_mode) / 32.0
        + jnp.einsum("tgqf,gfe->tgqe", query_features, past_linear_v, precision=exact_mode) / 4.0
        + past_values[None, :, None, :]
    )
    denominator = (
        denominator
        + jnp.einsum("tgqk,gk->tgq", query_square, past_square_k, precision=exact_mode) / 32.0
        + jnp.einsum("tgqf,gf->tgq", query_features, past_linear_k, precision=exact_mode) / 4.0
        + past_count[None, :, None]
    )
    linear_out = numerator / denominator[..., None]
    head_out = (
        (linear_out + window_out)
        .astype(jnp.bfloat16)
        .reshape(tok_rows, kv_groups * GROUP * HEAD_DIM)
    )
    all_heads = lax.all_gather(head_out, "head", axis=1, tiled=True)
    proj_full = lax.all_gather(out_proj, "ctx", axis=0, tiled=True)
    projected = jnp.dot(all_heads, proj_full, preferred_element_type=jnp.float32)
    student_out = projected.astype(jnp.bfloat16)
    residual = student_out.astype(jnp.float32) - teacher.astype(jnp.float32)
    total_rows = tok_rows * ctx_count
    loss_value = lax.psum(jnp.sum(residual * residual), ("ctx", "head")) / (total_rows * D)
    d_student = (2.0 * residual / total_rows).astype(jnp.bfloat16)
    head_terms = lax.dot_general(
        d_student, proj_full, (((1,), (1,)), ((), ())), preferred_element_type=jnp.float32
    )
    head_grad = (
        lax.psum_scatter(head_terms.astype(jnp.bfloat16), "head", scatter_dimension=1, tiled=True)
        .astype(jnp.float32)
        .reshape(tok_rows, kv_groups, GROUP, HEAD_DIM)
    )
    numerator_grad = head_grad / denominator[..., None]
    denominator_grad = -jnp.sum(head_grad * linear_out, axis=-1) / denominator
    kernel_grad = (
        jnp.einsum("tgqe,sge->gqts", numerator_grad, value_float, precision=exact_mode)
        + jnp.transpose(denominator_grad, (1, 2, 0))[..., None]
    )
    inner_grad = jnp.where(causal, kernel_grad * (1.0 + qk_inner), 0.0) / 4.0
    query_grad = jnp.einsum("gqts,sgf->tgqf", inner_grad, key_features, precision=exact_mode)
    key_grad = jnp.einsum("gqts,tgqf->sgf", inner_grad, query_features, precision=exact_mode)
    query_square_grad = (
        jnp.einsum("tgqe,gke->tgqk", numerator_grad, past_square_v, precision=exact_mode)
        + denominator_grad[..., None] * past_square_k[None, :, None, :]
    ) / 32.0
    query_grad = (
        query_grad
        + (
            jnp.einsum("tgqe,gfe->tgqf", numerator_grad, past_linear_v, precision=exact_mode)
            + denominator_grad[..., None] * past_linear_k[None, :, None, :]
        )
        / 4.0
        + square_grad(query_square_grad, query_features)
    )
    own_back_square = jnp.einsum(
        "tgqk,tgqe->gke", query_square, numerator_grad, precision=exact_mode
    )
    own_back_linear = jnp.einsum(
        "tgqf,tgqe->gfe", query_features, numerator_grad, precision=exact_mode
    )
    own_den_square = jnp.einsum(
        "tgqk,tgq->gk", query_square, denominator_grad, precision=exact_mode
    )
    own_den_linear = jnp.einsum(
        "tgqf,tgq->gf", query_features, denominator_grad, precision=exact_mode
    )
    gathered_back = (
        lax.all_gather(own_back_square[None], "ctx", axis=0, tiled=True),
        lax.all_gather(own_back_linear[None], "ctx", axis=0, tiled=True),
        lax.all_gather(own_den_square[None], "ctx", axis=0, tiled=True),
        lax.all_gather(own_den_linear[None], "ctx", axis=0, tiled=True),
    )
    upper_select = jnp.arange(ctx_count) > ctx_index
    later_sums = tuple((masked_total(upper_select, member) for member in gathered_back))
    later_square, later_linear, later_den_square, later_den_linear = later_sums
    key_square_grad = (
        jnp.einsum("gke,sge->sgk", later_square, value_float, precision=exact_mode)
        + later_den_square[None]
    ) / 32.0
    key_grad = (
        key_grad
        + (
            jnp.einsum("gfe,sge->sgf", later_linear, value_float, precision=exact_mode)
            + later_den_linear[None]
        )
        / 4.0
        + square_grad(key_square_grad, key_features)
    )
    own_grad = jnp.einsum(
        "tgqe,tgqf->gef", query_heads.astype(jnp.float32), query_grad, precision=exact_mode
    ) + jnp.einsum("tge,tgf->gef", key_heads.astype(jnp.float32), key_grad, precision=exact_mode)
    feature_grad = lax.psum(own_grad, "ctx")
    return (student_out, loss_value, feature_grad)


def solution(mesh):
    return jax.shard_map(
        local,
        mesh=mesh,
        in_specs=(
            P("ctx", "head"),
            P("ctx", "head"),
            P("ctx", "head"),
            P("head", None, None),
            P("ctx", "head"),
            P("ctx", "head"),
        ),
        out_specs=(P("ctx", "head"), P(), P("head", None, None)),
        check_vma=False,
    )
```

profile of v0, /device:TPU:0, one launch (start us, length us, event | category | flops | bytes accessed | tf_op | source)
XLA Modules:
  0.0 652.8 jit_solution(9237488309166573956)
XLA Ops:
  9.4 5.4 collective-permute-start
  20.9 18.1 %all_gather.39 = f32[8,1,256]{2,1,0:T(1,128)S(1)} all-gather(f32[1,1,256]{2,1,0:T(1,128)S(1)} %broadcast_in_dim.148), channel_id=1, replica_groups=mesh['ctx'=8,'head'=4] {'ctx'}, dimensions={0}, use_global_device_ids=true | all-gather | bytes 9216 | tf_op jit(solution)/shard_map/all_gather | solution.py:109
  42.0 7.1 %fusion.108 = f32[1,512,8]{0,1,2:T(8,128)S(1)} fusion(f32[256,1,1]{0,1,2:T(1,128)S(1)} %bitcast.398, f32[512,8,256]{0,2,1:T(8,128)S(1)} %bitcast.367), kind=kOutput, calls=%fused_computation.168 | convolution fusion | flops 12582912 | bytes 4211712 | tf_op jit(solution)/shard_map/tgqk,gk->tgq/dot_general | solution.py:125
  53.9 18.1 %all-reduce.3 = (f32[128]{0:T(128)S(1)}, f32[8]{0:T(128)}) all-reduce(f32[128]{0:T(128)S(1)} %dynamic-update-slice, f32[8]{0:T(128)S(1)} %dynamic-update-slice.1), channel_id=5, replica_groups=mesh['ctx'=8,'head'=4] {'ctx'}, use_global_device_ids=true, to_apply=%add | all-reduce | flops 136 | bytes 1088
  72.8 3.4 fusion.89
  77.4 11.7 %fusion.7 = (f32[8,512]{1,0:T(8,128)S(1)}, f32[512,512,8]{1,0,2:T(8,128)}) fusion(pred[512,512]{0,1:T(8,128)(4,1)} %iota_compare_fusion, f32[512,8,16]{0,2,1:T(8,128)S(1)} %convolution_bitcast_fusion.2, f32[16,512]{1,0:T(8,128)} %copy-done.6), kind=kOutput, calls=%fused_computation.10 | convolution fusion | flops 417329152 | bytes 8962048 | tf_op jit(solution)/shard_map/tgqf,sgf->gqts/dot_general | solution.py:93
  89.8 31.0 %all-gather.1 = f32[128,128]{1,0:T(8,128)S(1)} all-gather(f32[16,128]{1,0:T(8,128)S(1)} %fusion.93), channel_id=3, replica_groups=mesh['ctx'=8,'head'=4] {'ctx'}, dimensions={0}, use_global_device_ids=true | all-gather | bytes 73728 | tf_op jit(solution)/shard_map/all_gather | solution.py:107
  124.1 9.7 %fusion.5 = f32[8,512,128]{1,2,0:T(8,128)} fusion(f32[512,512,8]{1,0,2:T(8,128)} %get-tuple-element.13, pred[512,512]{0,1:T(8,128)(4,1)S(1)} %copy-done.17, bf16[512,128]{1,0:T(8,128)(2,1)S(1)} %copy-done.5), kind=kOutput, calls=%fused_computation.7 | convolution fusion | flops 3233808384 | bytes 10878976 | tf_op jit(solution)/shard_map/gqts,sge->tgqe/dot_general | solution.py:96
  135.2 18.2 %all-gather.8 = f32[8,1,128]{2,1,0:T(1,128)S(1)} all-gather(f32[1,1,128]{2,1,0:T(1,128)S(1)} %bitcast.399), channel_id=4, replica_groups=mesh['ctx'=8,'head'=4] {'ctx'}, dimensions={0}, use_global_device_ids=true | all-gather | bytes 4608 | tf_op jit(solution)/shard_map/all_gather | solution.py:108
  164.3 8.5 %add_convert_fusion = (bf16[512,1,8,128]{0,3,2,1:T(8,128)(2,1)}, f32[512,1,8,128]{0,3,2,1:T(8,128)}) fusion(f32[512,1,8,128]{0,3,2,1:T(8,128)} %copy.53, f32[512,8]{0,1:T(8,128)} %bitcast.390, f32[128]{0:T(128)S(1)} %copy-done.26, f32[128,512,8]{1,0,2:T(8,128)} %fusion.80, f32[512,8,256]{0,2,1:T(8,128)} %bitcast.368, ...), kind=kOutput, calls=%fused_computation.38 | convolution fusion | flops 1614807040 | bytes 13779456 | tf_op jit(solution)/shard_map/tgqk,gke->tgqe/dot_general | solution.py:119
  173.8 30.9 %all-gather.15.cloned.1.call-done = bf16[512,4096]{0,1:T(8,128)(2,1)} async-done(((bf16[512,1024]{0,1:T(8,128)(2,1)}), bf16[512,4096]{0,1:T(8,128)(2,1)}) %all-gather.15.cloned.1.call-update) | async-done | bytes 4194320 | tf_op jit(solution)/shard_map/all_gather | solution.py:135
  204.8 229.8 %all-gather.17.cloned.1.call-done = bf16[4096,2048]{1,0:T(8,128)(2,1)} async-done(((bf16[512,2048]{1,0:T(8,128)(2,1)}), bf16[4096,2048]{1,0:T(8,128)(2,1)}) %all-gather.17.cloned.1.call-update) | async-done | bytes 16777232 | tf_op jit(solution)/shard_map/all_gather | solution.py:136
  434.6 14.8 %multiply_reduce_fusion.2 = (f32[]{:T(128)}, bf16[512,2048]{1,0:T(8,128)(2,1)S(1)}) fusion(bf16[512,2048]{1,0:T(8,128)(2,1)S(1)} %copy-done.28, bf16[512,4096]{0,1:T(8,128)(2,1)} %all-gather.15.cloned.1.call-done, bf16[4096,2048]{1,0:T(8,128)(2,1)} %all-gather.17.cloned.1.call-done), kind=kOutput, calls=%fused_computation.16 | convolution fusion | flops 8596226048 | bytes 25165828 | tf_op jit(solution)/shard_map/dot_general | solution.py:137
  450.7 13.8 %convolution_convert_fusion = bf16[512,4096]{1,0:T(8,128)(2,1)} fusion(bf16[4096,2048]{1,0:T(8,128)(2,1)} %all-gather.17.cloned.1.call-done, bf16[512,2048]{1,0:T(8,128)(2,1)S(1)} %copy-done.28, bf16[512,2048]{1,0:T(8,128)(2,1)S(1)} %get-tuple-element.21), kind=kOutput, calls=%fused_computation.9 | convolution fusion | flops 8597274624 | bytes 25165824 | tf_op jit(solution)/shard_map/dot_general | solution.py:143
  466.0 39.3 %psum.14 = f32[]{:T(128)} all-reduce(f32[]{:T(128)} %get-tuple-element.20), channel_id=1, replica_groups=mesh['ctx'=8,'head'=4] {'ctx','head'}, use_global_device_ids=true, to_apply=%region_13.14 | all-reduce | flops 1 | bytes 8 | tf_op jit(solution)/shard_map/psum | solution.py:141
  516.1 4.3 convolution_bitcast_fusion.3
  520.4 20.5 %all-gather.9 = f32[8,1,256]{2,1,0:T(1,128)S(1)} all-gather(f32[1,1,256]{2,1,0:T(1,128)S(1)} %convolution_bitcast_fusion.7), channel_id=9, replica_groups=mesh['ctx'=8,'head'=4] {'ctx'}, dimensions={0}, use_global_device_ids=true | all-gather | bytes 9216 | tf_op jit(solution)/shard_map/all_gather | solution.py:188
  542.4 30.8 %all-gather.4 = f32[128,128]{1,0:T(8,128)S(1)} all-gather(f32[16,128]{1,0:T(8,128)S(1)} %convolution_bitcast_fusion.6), channel_id=6, replica_groups=mesh['ctx'=8,'head'=4] {'ctx'}, dimensions={0}, use_global_device_ids=true | all-gather | bytes 73728 | tf_op jit(solution)/shard_map/all_gather | solution.py:187
  573.6 17.3 %all-reduce.2 = f32[128]{0:T(128)S(1)} all-reduce(f32[128]{0:T(128)S(1)} %dynamic-update-slice.2), channel_id=7, replica_groups=mesh['ctx'=8,'head'=4] {'ctx'}, use_global_device_ids=true, to_apply=%add.2 | all-reduce | flops 128 | bytes 1024
  591.7 4.1 fusion.9
  600.0 10.8 %fusion.3 = f32[8,512,512]{1,2,0:T(8,128)S(1)} fusion(f32[512,512,8]{1,0,2:T(8,128)S(1)} %bitcast.401, f32[8,512]{1,0:T(8,128)S(1)} %get-tuple-element.7, pred[512,512]{0,1:T(8,128)(4,1)S(1)} %copy-done.18, bf16[512,128]{1,0:T(8,128)(2,1)S(1)} %copy-done.5, f32[64,8,8,128]{3,2,1,0:T(8,128)S(1)} %bitcast.380, bf16[512,1024]{1,0:T(8,128)(2,1)S(1)} %copy-done.10), kind=kOutput, calls=%fused_computation.4 | convolution fusion | flops 3234856960 | bytes 20332544 | tf_op jit(solution)/shard_map/tgqe,sge->gqts/dot_general | solution.py:154
  610.8 4.0 fusion.31
  615.5 7.1 %convolution_bitcast_fusion.4 = f32[512,1,16]{0,2,1:T(8,128)S(1)} fusion(f32[512,8,16]{0,2,1:T(8,128)S(1)} %convolution_bitcast_fusion.2, f32[8,512,512]{1,2,0:T(8,128)S(1)} %fusion.3), kind=kOutput, calls=%fused_computation.65 | convolution fusion | flops 402653184 | bytes 8683520 | tf_op jit(solution)/shard_map/gqts,tgqf->sgf/dot_general | solution.py:159
  624.9 20.0 %psum.15 = f32[1,128,16]{1,2,0:T(8,128)} all-reduce(f32[1,128,16]{1,2,0:T(8,128)S(1)} %fusion.46), channel_id=1, replica_groups=mesh['ctx'=8,'head'=4] {'ctx'}, use_global_device_ids=true, to_apply=%region_20.21 | all-reduce | flops 2048 | bytes 16384 | tf_op jit(solution)/shard_map/psum | solution.py:210
  (146 shorter events, 57.1 us)
Async XLA Ops:
  7.2 12.8 %copy-start.5 = (bf16[512,128]{1,0:T(8,128)(2,1)S(1)}, bf16[512,128]{1,0:T(8,128)(2,1)}, u32[]{:S(2)}) copy-start(bf16[512,128]{1,0:T(8,128)(2,1)} %param.8) | copy-start | bytes 393220
  7.2 31.8 %copy-start.4 = (bf16[512,1024]{1,0:T(8,128)(2,1)S(1)}, bf16[512,1024]{1,0:T(8,128)(2,1)}, u32[]{:S(2)}) copy-start(bf16[512,1024]{1,0:T(8,128)(2,1)} %param.6) | copy-start | bytes 3145732
  7.2 155.7 %all-gather.19.cloned.1.call-start = ((), (), s32[]{:S(2)}) async-start(), calls=%async_computation.4 | async-start | bytes 1179648 | tf_op jit(solution)/shard_map/all_gather | solution.py:106
  9.4 145.0 %collective-permute-start = (bf16[2,64,128]{2,1,0:T(8,128)(2,1)}, bf16[2,64,128]{2,1,0:T(8,128)(2,1)}, u32[]{:S(2)}, u32[]{:S(2)}) collective-permute-start(bf16[2,64,128]{2,1,0:T(8,128)(2,1)} %pad_maximum_fusion.2), channel_id=1, source_target_pairs={{0,4},{4,8},{8,12},{12,16},{16,20},{20,24},{24,28},{1,5},{5,9},{9,... | collective-permute-start | bytes 98312 | tf_op jit(solution)/shard_map/ppermute | solution.py:17
  18.7 186.1 %all-gather.15.cloned.1.call-start = ((), (), s32[]{:S(2)}) async-start(), calls=%async_computation.1 | async-start | bytes 5242880 | tf_op jit(solution)/shard_map/all_gather | solution.py:135
  40.1 9.0 %copy-start.21 = (f32[256]{0:T(256)}, f32[256]{0:T(256)S(1)}, u32[]{:S(2)}) copy-start(f32[256]{0:T(256)S(1)} %fusion.82) | copy-start | bytes 3076
  77.4 11.7 %copy-start.30 = (f32[8]{0:T(128)S(1)}, f32[8]{0:T(128)}, u32[]{:S(2)}) copy-start(f32[8]{0:T(128)} %get-tuple-element.4) | copy-start | bytes 100
  89.2 34.9 %copy-start.17 = (pred[512,512]{0,1:T(8,128)(4,1)S(1)}, pred[512,512]{0,1:T(8,128)(4,1)}, u32[]{:S(2)}) copy-start(pred[512,512]{0,1:T(8,128)(4,1)} %iota_compare_fusion) | copy-start | bytes 786436
  124.1 9.8 %copy-start.19 = (f32[1,512,8]{1,2,0:T(8,128)S(1)}, f32[1,512,8]{1,2,0:T(8,128)}, u32[]{:S(2)}) copy-start(f32[1,512,8]{1,2,0:T(8,128)} %copy.68) | copy-start | bytes 49156
  124.1 9.8 %copy-start.20 = (f32[1,512,8]{1,2,0:T(8,128)S(1)}, f32[1,512,8]{1,2,0:T(8,128)}, u32[]{:S(2)}) copy-start(f32[1,512,8]{1,2,0:T(8,128)} %copy.69) | copy-start | bytes 49156
  124.1 11.1 %copy-start.25 = (f32[128]{0:T(128)S(1)}, f32[128]{0:T(128)}, u32[]{:S(2)}) copy-start(f32[128]{0:T(128)} %convert_reduce_fusion) | copy-start | bytes 1540
  124.1 29.3 %copy-start.27 = (s32[64]{0:T(128)S(1)}, s32[64]{0:T(128)}, u32[]{:S(2)}) copy-start(s32[64]{0:T(128)} %iota_add_fusion) | copy-start | bytes 772
  133.9 21.3 %copy-start.8 = (bf16[512,128]{1,0:T(8,128)(2,1)S(1)}, bf16[512,128]{1,0:T(8,128)(2,1)}, u32[]{:S(2)}) copy-start(bf16[512,128]{1,0:T(8,128)(2,1)} %param.7) | copy-start | bytes 393220
  164.3 8.5 %copy-start.12 = (f32[256,128]{1,0:T(8,128)}, f32[256,128]{1,0:T(8,128)S(1)}, u32[]{:S(2)}) copy-start(f32[256,128]{1,0:T(8,128)S(1)} %select_reduce_fusion.1) | copy-start | bytes 393220
  172.8 261.8 %copy-start.28 = (bf16[512,2048]{1,0:T(8,128)(2,1)S(1)}, bf16[512,2048]{1,0:T(8,128)(2,1)}, u32[]{:S(2)}) copy-start(bf16[512,2048]{1,0:T(8,128)(2,1)} %param.11) | copy-start | bytes 6291460
  172.8 261.7 %all-gather.17.cloned.1.call-start = ((), (), s32[]{:S(2)}) async-start(), calls=%async_computation.2 | async-start | bytes 18874368 | tf_op jit(solution)/shard_map/all_gather | solution.py:136
  173.6 334.4 %reduce-scatter.2.cloned.1.call-start = ((), (), s32[]{:S(2)}) async-start(), calls=%async_computation.3 | async-start | bytes 5242880 | tf_op jit(solution)/shard_map/reduce_scatter | solution.py:147
  464.5 158.1 %all-gather.21.cloned.1.call-start = ((), (), s32[]{:S(2)}) async-start(), calls=%async_computation.5 | async-start | bytes 1179648 | tf_op jit(solution)/shard_map/all_gather | solution.py:186
  516.1 24.8 %copy-start.16 = (f32[512,1,8]{0,2,1:T(8,128)S(1)}, f32[512,1,8]{0,2,1:T(8,128)}, u32[]{:S(2)}) copy-start(f32[512,1,8]{0,2,1:T(8,128)} %fusion.76) | copy-start | bytes 49156
  540.9 50.2 %copy-start.11 = (f32[512,8]{1,0:T(8,128)S(1)}, f32[512,8]{1,0:T(8,128)}, u32[]{:S(2)}) copy-start(f32[512,8]{1,0:T(8,128)} %copy.98) | copy-start | bytes 49156
  542.4 49.3 %copy-start.13 = (f32[256,128]{1,0:T(8,128)S(1)}, f32[256,128]{1,0:T(8,128)}, u32[]{:S(2)}) copy-start(f32[256,128]{1,0:T(8,128)} %copy-done.12) | copy-start | bytes 393220
  542.4 49.3 %copy-start.22 = (f32[256]{0:T(256)S(1)}, f32[256]{0:T(256)}, u32[]{:S(2)}) copy-start(f32[256]{0:T(256)} %copy-done.21) | copy-start | bytes 3076
  600.0 10.8 %copy-start.7 = (f32[16,512]{1,0:T(8,128)S(1)}, f32[16,512]{1,0:T(8,128)}, u32[]{:S(2)}) copy-start(f32[16,512]{1,0:T(8,128)} %copy-done.6) | copy-start | bytes 98308
  615.5 29.4 %copy-start.1 = (bf16[1,128,16]{1,2,0:T(8,128)(2,1)S(1)}, bf16[1,128,16]{1,2,0:T(8,128)(2,1)}, u32[]{:S(2)}) copy-start(bf16[1,128,16]{1,2,0:T(8,128)(2,1)} %param.9) | copy-start | bytes 12292
  (15 other events, 41.8 us)
Sparse Core Ops, SparseCore 0:
  18.8 40.0 all-gather.18
  173.0 31.7 all-gather.14
  206.9 227.6 all-gather.16
  464.6 43.3 reduce-scatter.1
  520.5 40.2 all-gather.20
where the time goes:
time: 660 us; the launch traced here: 653 us
  waiting for transfers between devices  264 us (40%)
  blocking collectives  213 us (32%)
  matrix products  119 us (18%)
  local copies, waits for them, and re-layouts  19.3 us (3%)
  between operations  16.9 us (3%)
  other arithmetic  14.9 us (2%)
    all_gather x1, waiting for transfers between devices, local(): proj_full = lax.all_gather(out_proj, 'ctx', axis=0, tiled=True)  230 us
    psum x1, blocking collectives, local(): lax.psum(jnp.sum(residual * residual), ('ctx', 'head')) / (total_rows * D)  39.3 us
    unnamed x2, blocking collectives  35.4 us
    all_gather x1, blocking collectives, local(): lax.all_gather(own_linear_v[None], 'ctx', axis=0, tiled=True)  31 us
    all_gather x1, waiting for transfers between devices, local(): all_heads = lax.all_gather(head_out, 'head', axis=1, tiled=True)  30.9 us
    all_gather x1, blocking collectives, local(): lax.all_gather(own_back_linear[None], 'ctx', axis=0, tiled=True)  30.8 us
    all_gather x1, blocking collectives, local(): lax.all_gather(own_den_square[None], 'ctx', axis=0, tiled=True)  20.5 us
    psum x1, blocking collectives, local(): feature_grad = lax.psum(own_grad, 'ctx')  20 us
  transfers between devices with their start and end apart: 6, of which 3 were waited for; matrix products, arithmetic and copies ran while one was open for 14% of the time, Pallas kernels for 0%

commit v1 on v0

--- a/solution.py
+++ b/solution.py
@@ -9,6 +9,27 @@
 GROUP = 8
 WIN = 64
 exact_mode = lax.Precision.HIGHEST
+
+
+def collect(x, axis, dim):
+    count, index, span = (lax.axis_size(axis), lax.axis_index(axis), x.shape[dim])
+    upward = [(i, (i + 1) % count) for i in range(count)]
+    backward = [(i, (i - 1) % count) for i in range(count)]
+    whole = jnp.zeros((*x.shape[:dim], count * span, *x.shape[dim + 1 :]), x.dtype)
+    whole = lax.dynamic_update_slice_in_dim(whole, x, index * span, axis=dim)
+    from_left = from_right = x
+    half = count // 2
+    for turn in range(1, half + 1):
+        from_left = lax.ppermute(from_left, axis, upward)
+        whole = lax.dynamic_update_slice_in_dim(
+            whole, from_left, (index - turn) % count * span, axis=dim
+        )
+        if turn < count - half:
+            from_right = lax.ppermute(from_right, axis, backward)
+            whole = lax.dynamic_update_slice_in_dim(
+                whole, from_right, (index + turn) % count * span, axis=dim
+            )
+    return whole
 
 
 def shifted(block, axis, distance):
@@ -133,7 +154,7 @@
         .reshape(tok_rows, kv_groups * GROUP * HEAD_DIM)
     )
     all_heads = lax.all_gather(head_out, "head", axis=1, tiled=True)
-    proj_full = lax.all_gather(out_proj, "ctx", axis=0, tiled=True)
+    proj_full = collect(out_proj, "ctx", 0)
     projected = jnp.dot(all_heads, proj_full, preferred_element_type=jnp.float32)
     student_out = projected.astype(jnp.bfloat16)
     residual = student_out.astype(jnp.float32) - teacher.astype(jnp.float32)

time: 660 us -> 690 us (1.045)
  waiting for transfers between devices: 264 us -> 179 us
  blocking collectives: 213 us -> 293 us
  local copies, waits for them, and re-layouts: 19.3 us -> 47.5 us
  starting transfers between devices: 5.85 us -> 17.4 us
    all_gather x1 -> x0, waiting for transfers between devices: 230 us -> none  [local(): proj_full = lax.all_gather(out_proj, 'ctx', axis=0, tiled=True)]
    ppermute x0 -> x7, waiting for transfers between devices: none -> 176 us  [the longest x3 109 us: collect(): from_right = lax.ppermute(from_right, axis, backward)]
    all_gather x1, blocking collectives: 18.1 us -> 99.7 us  [local(): lax.all_gather(own_square_k[None], 'ctx', axis=0, tiled=True)]
    all_gather x1, waiting for transfers between devices: 30.9 us -> 0.01 us  [local(): all_heads = lax.all_gather(head_out, 'head', axis=1, tiled=True)]
    dynamic_update_slice x0 -> x8, local copies, waits for them, and re-layouts: none -> 22.2 us  [the longest x4 11.2 us: collect(): lax.dynamic_update_slice_in_dim(whole, from_left, (index - turn) % count...]
    ppermute x0 -> x7, starting transfers between devices: none -> 15.3 us  [the longest x3 7.82 us: collect(): from_right = lax.ppermute(from_right, axis, backward)]
  transfers between devices with their start and end apart: 6 -> 12, of which waited for: 3 -> 4; matrix products, arithmetic and copies ran while one was open for 14% -> 19% of each run, Pallas kernels for 0% -> 0%
where the time goes in v1:
time: 690 us; the launch traced here: 682 us
  blocking collectives  293 us (42%)
  waiting for transfers between devices  179 us (26%)
  matrix products  113 us (16%)
  local copies, waits for them, and re-layouts  47.5 us (7%)
  starting transfers between devices  17.4 us (3%)
  between operations  16.9 us (2%)
  other arithmetic  14.8 us (2%)
    ppermute x3, waiting for transfers between devices, collect(): from_right = lax.ppermute(from_right, axis, backward)  109 us
    all_gather x1, blocking collectives, local(): lax.all_gather(own_square_k[None], 'ctx', axis=0, tiled=True)  99.7 us
    ppermute x4, waiting for transfers between devices, collect(): from_left = lax.ppermute(from_left, axis, upward)  67.5 us
    psum x1, blocking collectives, local(): lax.psum(jnp.sum(residual * residual), ('ctx', 'head')) / (total_rows * D)  37.7 us
    unnamed x2, blocking collectives  35.4 us
    all_gather x1, blocking collectives, local(): lax.all_gather(own_back_linear[None], 'ctx', axis=0, tiled=True)  30.8 us
    all_gather x1, blocking collectives, local(): lax.all_gather(own_linear_v[None], 'ctx', axis=0, tiled=True)  30.6 us
    all_gather x1, blocking collectives, local(): lax.all_gather(own_den_square[None], 'ctx', axis=0, tiled=True)  20.5 us
  transfers between devices with their start and end apart: 12, of which 4 were waited for; matrix products, arithmetic and copies ran while one was open for 19% of the time, Pallas kernels for 0%

profile of v1, /device:TPU:0, one launch (start us, length us, event | category | flops | bytes accessed | tf_op | source)
XLA Modules:
  0.0 681.9 jit_solution(15124361298389968121)
XLA Ops:
  23.3 99.7 %all_gather.36 = f32[8,1,256]{2,1,0:T(1,128)S(1)} all-gather(f32[1,1,256]{2,1,0:T(1,128)S(1)} %broadcast_in_dim.151), channel_id=1, replica_groups=mesh['ctx'=8,'head'=4] {'ctx'}, dimensions={0}, use_global_device_ids=true | all-gather | bytes 9216 | tf_op jit(solution)/shard_map/all_gather | solution.py:130
  126.0 7.1 %fusion.108 = f32[1,512,8]{0,1,2:T(8,128)S(1)} fusion(f32[256,1,1]{0,1,2:T(1,128)S(1)} %bitcast.398, f32[512,8,256]{0,2,1:T(8,128)S(1)} %bitcast.367), kind=kOutput, calls=%fused_computation.176 | convolution fusion | flops 12582912 | bytes 4211712 | tf_op jit(solution)/shard_map/tgqk,gk->tgq/dot_general | solution.py:146
  137.9 18.1 %all-reduce.3 = (f32[128]{0:T(128)S(1)}, f32[8]{0:T(128)}) all-reduce(f32[128]{0:T(128)S(1)} %dynamic-update-slice, f32[8]{0:T(128)S(1)} %dynamic-update-slice.1), channel_id=5, replica_groups=mesh['ctx'=8,'head'=4] {'ctx'}, use_global_device_ids=true, to_apply=%add | all-reduce | flops 136 | bytes 1088
  162.0 9.8 %fusion.7 = (f32[8,512]{1,0:T(8,128)S(1)}, f32[512,512,8]{1,0,2:T(8,128)S(1)}) fusion(pred[512,512]{0,1:T(8,128)(4,1)} %iota_compare_fusion, f32[512,8,16]{0,2,1:T(8,128)S(1)} %convolution_bitcast_fusion.2, f32[16,512]{1,0:T(8,128)} %copy-done.7), kind=kOutput, calls=%fused_computation.10 | convolution fusion | flops 417329152 | bytes 8962048 | tf_op jit(solution)/shard_map/tgqf,sgf->gqts/dot_general | solution.py:114
  171.9 30.6 %all-gather.1 = f32[128,128]{1,0:T(8,128)S(1)} all-gather(f32[16,128]{1,0:T(8,128)S(1)} %fusion.93), channel_id=3, replica_groups=mesh['ctx'=8,'head'=4] {'ctx'}, dimensions={0}, use_global_device_ids=true | all-gather | bytes 73728 | tf_op jit(solution)/shard_map/all_gather | solution.py:128
  205.8 6.1 fusion.5
  213.2 18.2 %all-gather.8 = f32[8,1,128]{2,1,0:T(1,128)S(1)} all-gather(f32[1,1,128]{2,1,0:T(1,128)S(1)} %bitcast.399), channel_id=4, replica_groups=mesh['ctx'=8,'head'=4] {'ctx'}, dimensions={0}, use_global_device_ids=true | all-gather | bytes 4608 | tf_op jit(solution)/shard_map/all_gather | solution.py:129
  242.4 8.5 %add_convert_fusion = (bf16[512,1,8,128]{0,3,2,1:T(8,128)(2,1)}, f32[512,1,8,128]{0,3,2,1:T(8,128)}) fusion(f32[512,1,8,128]{0,3,2,1:T(8,128)} %copy.53, f32[512,8]{0,1:T(8,128)} %bitcast.390, f32[128]{0:T(128)S(1)} %copy-done.27, f32[128,512,8]{1,0,2:T(8,128)} %fusion.80, f32[512,8,256]{0,2,1:T(8,128)} %bitcast.368, ...), kind=kOutput, calls=%fused_computation.38 | convolution fusion | flops 1614807040 | bytes 13779456 | tf_op jit(solution)/shard_map/tgqk,gke->tgqe/dot_general | solution.py:140
  251.0 4.7 collective-permute-start.4
  255.7 67.4 %collective-permute-done.3 = bf16[512,2048]{1,0:T(8,128)(2,1)S(1)} collective-permute-done((bf16[512,2048]{1,0:T(8,128)(2,1)}, bf16[512,2048]{1,0:T(8,128)(2,1)S(1)}, u32[]{:S(2)}, u32[]{:S(2)}) %collective-permute-start.3) | collective-permute-done | bytes 2097184 | tf_op jit(solution)/shard_map/ppermute | solution.py:23
  325.5 39.7 %collective-permute-done.4 = bf16[512,2048]{1,0:T(8,128)(2,1)} collective-permute-done((bf16[512,2048]{1,0:T(8,128)(2,1)}, bf16[512,2048]{1,0:T(8,128)(2,1)}, u32[]{:S(2)}, u32[]{:S(2)}) %collective-permute-start.4) | collective-permute-done | bytes 2097184 | tf_op jit(solution)/shard_map/ppermute | solution.py:28
  367.3 6.2 broadcast_in_dim.157
  389.0 69.0 %collective-permute-done.6 = bf16[512,2048]{1,0:T(8,128)(2,1)} collective-permute-done((bf16[512,2048]{1,0:T(8,128)(2,1)}, bf16[512,2048]{1,0:T(8,128)(2,1)}, u32[]{:S(2)}, u32[]{:S(2)}) %collective-permute-start.6) | collective-permute-done | bytes 2097184 | tf_op jit(solution)/shard_map/ppermute | solution.py:28
  464.6 14.8 %multiply_reduce_fusion.2 = (f32[]{:T(128)}, bf16[512,2048]{1,0:T(8,128)(2,1)S(1)}) fusion(bf16[512,2048]{1,0:T(8,128)(2,1)S(1)} %copy-done.29, bf16[512,4096]{0,1:T(8,128)(2,1)} %all-gather.14.cloned.1.call-done, bf16[4096,2048]{1,0:T(8,128)(2,1)} %constant_dynamic-update-slice_fusion), kind=kOutput, calls=%fused_computation.16 | convolution fusion | flops 8596226048 | bytes 25165828 | tf_op jit(solution)/shard_map/dot_general | solution.py:158
  480.7 13.8 %convolution_convert_fusion = bf16[512,4096]{1,0:T(8,128)(2,1)} fusion(bf16[4096,2048]{1,0:T(8,128)(2,1)} %constant_dynamic-update-slice_fusion, bf16[512,2048]{1,0:T(8,128)(2,1)S(1)} %copy-done.29, bf16[512,2048]{1,0:T(8,128)(2,1)S(1)} %get-tuple-element.21), kind=kOutput, calls=%fused_computation.9 | convolution fusion | flops 8597274624 | bytes 25165824 | tf_op jit(solution)/shard_map/dot_general | solution.py:164
  496.0 37.7 %psum.14 = f32[]{:T(128)} all-reduce(f32[]{:T(128)} %get-tuple-element.20), channel_id=1, replica_groups=mesh['ctx'=8,'head'=4] {'ctx','head'}, use_global_device_ids=true, to_apply=%region_13.14 | all-reduce | flops 1 | bytes 8 | tf_op jit(solution)/shard_map/psum | solution.py:162
  545.2 4.3 convolution_bitcast_fusion.3
  549.5 20.5 %all-gather.9 = f32[8,1,256]{2,1,0:T(1,128)S(1)} all-gather(f32[1,1,256]{2,1,0:T(1,128)S(1)} %convolution_bitcast_fusion.7), channel_id=9, replica_groups=mesh['ctx'=8,'head'=4] {'ctx'}, dimensions={0}, use_global_device_ids=true | all-gather | bytes 9216 | tf_op jit(solution)/shard_map/all_gather | solution.py:209
  571.5 30.8 %all-gather.4 = f32[128,128]{1,0:T(8,128)S(1)} all-gather(f32[16,128]{1,0:T(8,128)S(1)} %convolution_bitcast_fusion.6), channel_id=6, replica_groups=mesh['ctx'=8,'head'=4] {'ctx'}, dimensions={0}, use_global_device_ids=true | all-gather | bytes 73728 | tf_op jit(solution)/shard_map/all_gather | solution.py:208
  602.8 17.3 %all-reduce.2 = f32[128]{0:T(128)S(1)} all-reduce(f32[128]{0:T(128)S(1)} %dynamic-update-slice.2), channel_id=7, replica_groups=mesh['ctx'=8,'head'=4] {'ctx'}, use_global_device_ids=true, to_apply=%add.2 | all-reduce | flops 128 | bytes 1024
  620.8 4.1 fusion.9
  629.1 10.8 %fusion.3 = f32[8,512,512]{1,2,0:T(8,128)S(1)} fusion(f32[512,512,8]{1,0,2:T(8,128)S(1)} %bitcast.401, f32[8,512]{1,0:T(8,128)S(1)} %get-tuple-element.7, pred[512,512]{0,1:T(8,128)(4,1)S(1)} %copy-done.19, bf16[512,128]{1,0:T(8,128)(2,1)S(1)} %copy-done.5, f32[64,8,8,128]{3,2,1,0:T(8,128)S(1)} %bitcast.380, bf16[512,1024]{1,0:T(8,128)(2,1)S(1)} %copy-done.11), kind=kOutput, calls=%fused_computation.4 | convolution fusion | flops 3234856960 | bytes 20332544 | tf_op jit(solution)/shard_map/tgqe,sge->gqts/dot_general | solution.py:175
  644.6 7.1 %convolution_bitcast_fusion.4 = f32[512,1,16]{0,2,1:T(8,128)S(1)} fusion(f32[512,8,16]{0,2,1:T(8,128)S(1)} %convolution_bitcast_fusion.2, f32[8,512,512]{1,2,0:T(8,128)S(1)} %fusion.3), kind=kOutput, calls=%fused_computation.65 | convolution fusion | flops 402653184 | bytes 8683520 | tf_op jit(solution)/shard_map/gqts,tgqf->sgf/dot_general | solution.py:180
  654.1 19.9 %psum.15 = f32[1,128,16]{1,2,0:T(8,128)} all-reduce(f32[1,128,16]{1,2,0:T(8,128)S(1)} %fusion.46), channel_id=1, replica_groups=mesh['ctx'=8,'head'=4] {'ctx'}, use_global_device_ids=true, to_apply=%region_20.21 | all-reduce | flops 2048 | bytes 16384 | tf_op jit(solution)/shard_map/psum | solution.py:231
  (170 shorter events, 98.8 us)
Async XLA Ops:
  7.2 15.3 %copy-start.5 = (bf16[512,128]{1,0:T(8,128)(2,1)S(1)}, bf16[512,128]{1,0:T(8,128)(2,1)}, u32[]{:S(2)}) copy-start(bf16[512,128]{1,0:T(8,128)(2,1)} %param.8) | copy-start | bytes 393220
  7.2 115.8 %copy-start.4 = (bf16[512,1024]{1,0:T(8,128)(2,1)S(1)}, bf16[512,1024]{1,0:T(8,128)(2,1)}, u32[]{:S(2)}) copy-start(bf16[512,1024]{1,0:T(8,128)(2,1)} %param.6) | copy-start | bytes 3145732
  7.2 233.7 %all-gather.16.cloned.1.call-start = ((), (), s32[]{:S(2)}) async-start(), calls=%async_computation.3 | async-start | bytes 1179648 | tf_op jit(solution)/shard_map/all_gather | solution.py:127
  7.2 235.0 %collective-permute-start.1 = (bf16[512,2048]{1,0:T(8,128)(2,1)}, bf16[512,2048]{1,0:T(8,128)(2,1)}, u32[]{:S(2)}, u32[]{:S(2)}) collective-permute-start(bf16[512,2048]{1,0:T(8,128)(2,1)} %param.10), channel_id=1, source_target_pairs={{0,4},{4,8},{8,12},{12,16},{16,20},{20,24},{24,28},{28,0},{1,5},{5... | collective-permute-start | bytes 6291464 | tf_op jit(solution)/shard_map/ppermute | solution.py:23
  10.2 240.7 %collective-permute-start.2 = (bf16[512,2048]{1,0:T(8,128)(2,1)}, bf16[512,2048]{1,0:T(8,128)(2,1)}, u32[]{:S(2)}, u32[]{:S(2)}) collective-permute-start(bf16[512,2048]{1,0:T(8,128)(2,1)} %param.10), channel_id=1, source_target_pairs={{0,28},{4,0},{8,4},{12,8},{16,12},{20,16},{24,20},{28,24},{1,29},{... | collective-permute-start | bytes 6291464 | tf_op jit(solution)/shard_map/ppermute | solution.py:28
  15.4 216.9 %collective-permute-start = (bf16[2,64,128]{2,1,0:T(8,128)(2,1)}, bf16[2,64,128]{2,1,0:T(8,128)(2,1)}, u32[]{:S(2)}, u32[]{:S(2)}) collective-permute-start(bf16[2,64,128]{2,1,0:T(8,128)(2,1)} %pad_maximum_fusion.2), channel_id=1, source_target_pairs={{0,4},{4,8},{8,12},{12,16},{16,20},{20,24},{24,28},{1,5},{5,9},{9,... | collective-permute-start | bytes 98312 | tf_op jit(solution)/shard_map/ppermute | solution.py:38
  21.1 443.5 %all-gather.14.cloned.1.call-start = ((), (), s32[]{:S(2)}) async-start(), calls=%async_computation.1 | async-start | bytes 5242880 | tf_op jit(solution)/shard_map/all_gather | solution.py:156
  171.9 40.0 %copy-start.32 = (f32[512,512,8]{1,0,2:T(8,128)}, f32[512,512,8]{1,0,2:T(8,128)S(1)}, u32[]{:S(2)}) copy-start(f32[512,512,8]{1,0,2:T(8,128)S(1)} %get-tuple-element.13) | copy-start | bytes 25165828
  171.9 33.9 %copy-start.18 = (pred[512,512]{0,1:T(8,128)(4,1)S(1)}, pred[512,512]{0,1:T(8,128)(4,1)}, u32[]{:S(2)}) copy-start(pred[512,512]{0,1:T(8,128)(4,1)} %iota_compare_fusion) | copy-start | bytes 786436
  205.8 25.5 %copy-start.28 = (s32[64]{0:T(128)S(1)}, s32[64]{0:T(128)}, u32[]{:S(2)}) copy-start(s32[64]{0:T(128)} %iota_add_fusion) | copy-start | bytes 772
  211.9 21.2 %copy-start.9 = (bf16[512,128]{1,0:T(8,128)(2,1)S(1)}, bf16[512,128]{1,0:T(8,128)(2,1)}, u32[]{:S(2)}) copy-start(bf16[512,128]{1,0:T(8,128)(2,1)} %param.7) | copy-start | bytes 393220
  242.3 80.9 %collective-permute-start.3 = (bf16[512,2048]{1,0:T(8,128)(2,1)}, bf16[512,2048]{1,0:T(8,128)(2,1)S(1)}, u32[]{:S(2)}, u32[]{:S(2)}) collective-permute-start(bf16[512,2048]{1,0:T(8,128)(2,1)} %collective-permute-done.1), channel_id=1, source_target_pairs={{0,4},{4,8},{8,12},{12,16},{16,20},{20,24},{24,28},{28,0},{1,5},{5... | collective-permute-start | bytes 6291464 | tf_op jit(solution)/shard_map/ppermute | solution.py:23
  250.9 286.2 %reduce-scatter.2.cloned.1.call-start = ((), (), s32[]{:S(2)}) async-start(), calls=%async_computation.2 | async-start | bytes 5242880 | tf_op jit(solution)/shard_map/reduce_scatter | solution.py:168
  251.0 114.2 %collective-permute-start.4 = (bf16[512,2048]{1,0:T(8,128)(2,1)}, bf16[512,2048]{1,0:T(8,128)(2,1)}, u32[]{:S(2)}, u32[]{:S(2)}) collective-permute-start(bf16[512,2048]{1,0:T(8,128)(2,1)} %collective-permute-done.2), channel_id=1, source_target_pairs={{0,28},{4,0},{8,4},{12,8},{16,12},{20,16},{24,20},{28,24},{1,29},{... | collective-permute-start | bytes 6291464 | tf_op jit(solution)/shard_map/ppermute | solution.py:28
  323.1 42.1 %collective-permute-start.5 = (bf16[512,2048]{1,0:T(8,128)(2,1)S(1)}, bf16[512,2048]{1,0:T(8,128)(2,1)}, u32[]{:S(2)}, u32[]{:S(2)}) collective-permute-start(bf16[512,2048]{1,0:T(8,128)(2,1)S(1)} %collective-permute-done.3), channel_id=1, source_target_pairs={{0,4},{4,8},{8,12},{12,16},{16,20},{20,24},{24,28},{28,0},{1,5},{5... | collective-permute-start | bytes 6291464 | tf_op jit(solution)/shard_map/ppermute | solution.py:23
  365.2 92.8 %collective-permute-start.6 = (bf16[512,2048]{1,0:T(8,128)(2,1)}, bf16[512,2048]{1,0:T(8,128)(2,1)}, u32[]{:S(2)}, u32[]{:S(2)}) collective-permute-start(bf16[512,2048]{1,0:T(8,128)(2,1)} %collective-permute-done.4), channel_id=1, source_target_pairs={{0,28},{4,0},{8,4},{12,8},{16,12},{20,16},{24,20},{28,24},{1,29},{... | collective-permute-start | bytes 6291464 | tf_op jit(solution)/shard_map/ppermute | solution.py:28
  365.2 96.0 %collective-permute-start.7 = (bf16[512,2048]{1,0:T(8,128)(2,1)}, bf16[512,2048]{1,0:T(8,128)(2,1)}, u32[]{:S(2)}, u32[]{:S(2)}) collective-permute-start(bf16[512,2048]{1,0:T(8,128)(2,1)} %collective-permute-done.5), channel_id=1, source_target_pairs={{0,4},{4,8},{8,12},{12,16},{16,20},{20,24},{24,28},{28,0},{1,5},{5... | collective-permute-start | bytes 6291464 | tf_op jit(solution)/shard_map/ppermute | solution.py:23
  494.5 157.2 %all-gather.18.cloned.1.call-start = ((), (), s32[]{:S(2)}) async-start(), calls=%async_computation.4 | async-start | bytes 1179648 | tf_op jit(solution)/shard_map/all_gather | solution.py:207
  545.2 24.8 %copy-start.17 = (f32[512,1,8]{0,2,1:T(8,128)S(1)}, f32[512,1,8]{0,2,1:T(8,128)}, u32[]{:S(2)}) copy-start(f32[512,1,8]{0,2,1:T(8,128)} %fusion.76) | copy-start | bytes 49156
  570.0 50.2 %copy-start.12 = (f32[512,8]{1,0:T(8,128)S(1)}, f32[512,8]{1,0:T(8,128)}, u32[]{:S(2)}) copy-start(f32[512,8]{1,0:T(8,128)} %copy.98) | copy-start | bytes 49156
  571.5 49.3 %copy-start.14 = (f32[256,128]{1,0:T(8,128)S(1)}, f32[256,128]{1,0:T(8,128)}, u32[]{:S(2)}) copy-start(f32[256,128]{1,0:T(8,128)} %copy-done.13) | copy-start | bytes 393220
  571.5 49.3 %copy-start.23 = (f32[256]{0:T(256)S(1)}, f32[256]{0:T(256)}, u32[]{:S(2)}) copy-start(f32[256]{0:T(256)} %copy-done.22) | copy-start | bytes 3076
  629.1 10.8 %copy-start.8 = (f32[16,512]{1,0:T(8,128)S(1)}, f32[16,512]{1,0:T(8,128)}, u32[]{:S(2)}) copy-start(f32[16,512]{1,0:T(8,128)} %copy-done.7) | copy-start | bytes 98308
  644.6 29.4 %copy-start.1 = (bf16[1,128,16]{1,2,0:T(8,128)(2,1)S(1)}, bf16[1,128,16]{1,2,0:T(8,128)(2,1)}, u32[]{:S(2)}) copy-start(bf16[1,128,16]{1,2,0:T(8,128)(2,1)} %param.9) | copy-start | bytes 12292
  (23 other events, 95.8 us)
Sparse Core Ops, SparseCore 0:
  21.2 74.2 all-gather.15
  251.1 35.8 all-gather.13
  494.6 42.4 reduce-scatter.1
  549.6 40.2 all-gather.17
